TPU v7x, 256 devices: a whole 4x4x8 slice. The times are simulated.
256 devices in a mesh: tm: 8 (over y, x_hi), lon: 32 (over x_lo, z, core).
Axes of the slice: x: 4 (x_hi: 2, x_lo: 2; x = x_hi * 2 + x_lo), y: 4, z: 8, core: 2. Of those that a mesh axis runs over, the one named last changes fastest.
Arguments:
- frames: bfloat16 [64, 16, 24, 4096], P(None, 'tm', None, 'lon'), may hold values from -6 to 6
- cotangent: bfloat16 [64, 16, 24, 4096], P(None, 'tm', None, 'lon'), may hold values from -6 to 6
- w_space: bfloat16 [3, 3, 64, 64], replicated, may hold values from -0.25 to 0.25
- w_time: bfloat16 [3, 64, 64], replicated, may hold values from -0.4375 to 0.4375
Outputs:
- grad_frames: bfloat16 [64, 16, 24, 4096], P(None, 'tm', None, 'lon')
- grad_space: float32 [3, 3, 64, 64], replicated
- grad_time: float32 [3, 64, 64], replicated
All inputs are finite; a program needn't handle non-finite values.
Results may differ from a plain program's by a relative error of at most 0.0049.
Values may be sent and summed in bfloat16 or wider, within the bound.
No kernel may reach another device: no remote copies, remote signals or barrier semaphores. Data moves between devices by JAX's collectives and lax.ppermute only.
A program may use at most 64 MiB of HBM per device.

v0:
```python
import math
import jax
import jax.numpy as jnp
from jax import lax
from jax.sharding import PartitionSpec as P


def padded_2(cells, sides, width):
    for axis, dim in sides:
        count = lax.axis_size(axis)
        head = lax.slice_in_dim(cells, 0, width, axis=dim)
        tail = lax.slice_in_dim(cells, cells.shape[dim] - width, cells.shape[dim], axis=dim)
        cells = jnp.concatenate(
            [
                lax.ppermute(tail, axis, [(i, (i + 1) % count) for i in range(count)]),
                cells,
                lax.ppermute(head, axis, [((i + 1) % count, i) for i in range(count)]),
            ],
            axis=dim,
        )
    return cells


def from_behind(value, axis, steps):
    count = lax.axis_size(axis)
    first, last = (max(0, -steps), min(count, count - steps))
    return lax.ppermute(value, axis, [(source, source + steps) for source in range(first, last)])


def silu_slope(pre):
    sigmoid_value = jax.nn.sigmoid(pre)
    return sigmoid_value * (1.0 + pre * (1.0 - sigmoid_value))


def pad_rows(field):
    return jnp.pad(field, ((0, 0), (0, 0), (1, 1), (0, 0)))


def body(frames, cotangent, w_space, w_time):
    channels, frame_count, lat_rows, lon_cols = frames.shape
    contract_last = (((1,), (1,)), ((), ()))
    contract_first = (((0,), (0,)), ((), ()))
    padded = pad_rows(padded_2(frames, (("lon", 3),), 1))
    later_frames = from_behind(cotangent, "tm", -1)
    later_ext = jnp.concatenate([cotangent, later_frames], axis=1)
    pre = None
    for i in range(3):
        for j in range(3):
            window = padded[:, :, i : i + lat_rows, j : j + lon_cols].reshape(channels, -1)
            term = jnp.dot(w_space[i, j], window, preferred_element_type=jnp.float32)
            pre = term if pre is None else pre + term
    act = jax.nn.silu(pre).astype(jnp.bfloat16)
    upstream = None
    for k in range(3):
        later_k = later_ext[:, k : k + frame_count].reshape(channels, -1)
        term = lax.dot_general(
            w_time[k], later_k, contract_first, preferred_element_type=jnp.float32
        )
        upstream = term if upstream is None else upstream + term
    tm_terms = []
    act_grid = act.reshape(channels, frame_count, lat_rows, lon_cols)
    earlier = from_behind(act_grid, "tm", 1)
    act_ext = jnp.concatenate([earlier, act_grid], axis=1)
    cot_flat = cotangent.reshape(channels, -1)
    for k in range(3):
        window = act_ext[:, 2 - k : 2 - k + frame_count].reshape(channels, -1)
        tm_terms.append(
            lax.dot_general(cot_flat, window, contract_last, preferred_element_type=jnp.float32)
        )
    grad_tm = jnp.stack(tm_terms)
    dpre = (upstream * silu_slope(pre)).astype(jnp.bfloat16)
    dpre_grid = dpre.reshape(channels, frame_count, lat_rows, lon_cols)
    dpad = pad_rows(padded_2(dpre_grid, (("lon", 3),), 1))
    sp_terms = []
    for i in range(3):
        for j in range(3):
            window = padded[:, :, i : i + lat_rows, j : j + lon_cols].reshape(channels, -1)
            sp_terms.append(
                lax.dot_general(dpre, window, contract_last, preferred_element_type=jnp.float32)
            )
    grad_sp = jnp.stack(sp_terms).reshape(3, 3, channels, channels)
    back = None
    for i in range(3):
        for j in range(3):
            window = dpad[:, :, 2 - i : 2 - i + lat_rows, 2 - j : 2 - j + lon_cols].reshape(
                channels, -1
            )
            term = lax.dot_general(
                w_space[i, j], window, contract_first, preferred_element_type=jnp.float32
            )
            back = term if back is None else back + term
    grad_frames = back.astype(jnp.bfloat16).reshape(channels, frame_count, lat_rows, lon_cols)
    grad_sp, grad_tm = lax.psum((grad_sp, grad_tm), ("tm", "lon"))
    total_cells = frame_count * lax.axis_size("tm") * lat_rows * lon_cols * lax.axis_size("lon")
    scale = 1.0 / math.sqrt(total_cells)
    return (grad_frames, grad_sp * scale, grad_tm * scale)


def solution(mesh):
    return jax.shard_map(
        body,
        mesh=mesh,
        in_specs=(P(None, "tm", None, "lon"), P(None, "tm", None, "lon"), P(), P()),
        out_specs=(P(None, "tm", None, "lon"), P(), P()),
        check_vma=False,
    )
```

profile of v0, /device:TPU:1, one launch (start us, length us, event | category | flops | bytes accessed | tf_op | source)
XLA Modules:
  0.0 309.6 jit_solution(8349422694415326540)
XLA Ops:
  7.2 1.7 fusion.141
  9.0 0.7 copy.31
  9.7 3.1 collective-permute-start.1
  12.7 0.7 copy.32
  13.7 1.5 collective-permute-start
  15.2 0.7 copy.14
  15.9 0.7 collective-permute-done.2
  16.6 0.7 copy.15
  17.3 1.9 fusion.13
  19.1 0.9 pad_maximum_fusion.3
  20.0 1.8 fusion.139
  24.7 0.8 multiply_convert_fusion
  25.6 1.1 copy.24
  26.7 5.7 %collective-permute-start.5 = (bf16[64,2,24,128]{3,0,2,1:T(8,128)(2,1)}, bf16[64,2,24,128]{3,0,2,1:T(8,128)(2,1)}, u32[]{:S(2)}, u32[]{:S(2)}) collective-permute-start(bf16[64,2,24,128]{3,0,2,1:T(8,128)(2,1)} %copy.24), channel_id=1, source_target_pairs={{0,32},{32,64},{64,96},{96,128},{128,160},{160,192},{192,224},{1,3... | collective-permute-start | bytes 2359304 | tf_op jit(solution)/shard_map/ppermute | solution.py:27
  32.8 1.1 pad_maximum_fusion.4
  33.9 0.4 convolution_bitcast_fusion.4
  34.7 1.9 fusion.7
  40.0 0.7 copy-done.10
  40.7 0.7 copy.33
  41.4 5.8 %collective-permute-start.3 = (bf16[64,2,24,1]{0,2,3,1:T(8,128)(2,1)S(1)}, bf16[64,2,24,1]{0,2,3,1:T(8,128)(2,1)S(1)}, u32[]{:S(2)}, u32[]{:S(2)}) collective-permute-start(bf16[64,2,24,1]{0,2,3,1:T(8,128)(2,1)S(1)} %copy.33), channel_id=1, source_target_pairs={{0,1},{1,2},{2,3},{3,4},{4,5},{5,6},{6,7},{7,8},{8,9},{9,10},{10,1... | collective-permute-start | bytes 18440 | tf_op jit(solution)/shard_map/ppermute | solution.py:15
  47.2 0.7 copy.34
  47.9 2.1 fusion.19
  50.1 0.7 copy.20
  50.8 0.6 collective-permute-done.4
  51.3 0.7 copy.21
  52.0 0.9 copy-done.2
  52.9 2.0 pad_maximum_fusion
  54.9 3.3 %select_maximum_fusion = bf16[64,2,26,130]{3,2,1,0:T(8,128)(2,1)S(1)} fusion(bf16[64,2,24,1]{3,2,1,0:T(8,128)(2,1)} %copy-done.2, bf16[64,2,24,128]{3,2,1,0:T(8,128)(2,1)S(1)} %bitcast.272, bf16[64,2,24,1]{3,2,1,0:T(8,128)(2,1)} %copy-done.1), kind=kLoop, calls=%fused_computation.30 | loop fusion | flops 5191680 | bytes 1664000 | tf_op jit(solution)/shard_map/concatenate | solution.py:13
  58.3 1.5 fusion.28
  59.7 1.5 convolution_bitcast_fusion.5
  61.3 82.8 %psum.15 = f32[3,64,64]{1,2,0:T(8,128)S(1)} all-reduce(f32[3,64,64]{1,2,0:T(8,128)S(1)} %pad_maximum_fusion.5), channel_id=1, replica_groups=mesh['tm'=8,'lon'=32] {'tm','lon'}, use_global_device_ids=true, to_apply=%region_1.2 | all-reduce | flops 12288 | bytes 98304 | tf_op jit(solution)/shard_map/psum | solution.py:93
  144.1 1.8 fusion.138
  145.8 0.4 fusion.45
  146.2 0.4 convolution_add_fusion.10
  146.7 0.4 convolution_add_fusion.9
  147.1 0.7 copy-done.8
  147.8 0.4 convolution_add_fusion.8
  148.2 0.7 copy-done.4
  148.9 0.4 convolution_add_fusion.7
  149.4 0.7 copy-done.7
  150.1 0.4 convolution_add_fusion.6
  150.5 0.4 convolution_add_fusion.5
  150.9 0.4 convolution_add_fusion.4
  151.3 0.4 fusion.18
  151.8 0.7 copy.28
  152.5 1.0 copy.56
  153.5 147.6 %all-reduce.4.cloned.1.call-done = f32[3,3,64,64]{3,2,1,0:T(8,128)} async-done(((f32[3,3,64,64]{3,2,1,0:T(8,128)}), f32[3,3,64,64]{3,2,1,0:T(8,128)}) %all-reduce.4.cloned.1.call-update) | async-done | bytes 147472 | tf_op jit(solution)/shard_map/psum | solution.py:93
  301.1 1.7 broadcast_multiply_fusion
  (50 shorter events, 7.5 us)
Async XLA Ops:
  7.2 293.9 %all-reduce.4.cloned.1.call-start = ((), (), s32[]{:S(2)}) async-start(), calls=%async_computation | async-start | bytes 589824 | tf_op jit(solution)/shard_map/psum | solution.py:93
  8.9 4.8 %copy-start.5 = (bf16[64,2,24,128]{3,2,1,0:T(8,128)(2,1)S(1)}, bf16[64,2,24,128]{3,2,1,0:T(8,128)(2,1)}, u32[]{:S(2)}) copy-start(bf16[64,2,24,128]{3,2,1,0:T(8,128)(2,1)} %param.5) | copy-start | bytes 2359300
  9.0 8.3 %copy-start = (bf16[64,2,24,128]{3,2,1,0:T(8,128)(2,1)S(1)}, bf16[64,2,24,128]{3,2,1,0:T(8,128)(2,1)}, u32[]{:S(2)}) copy-start(bf16[64,2,24,128]{3,2,1,0:T(8,128)(2,1)} %param.4) | copy-start | bytes 2359300
  9.7 5.5 %collective-permute-start.1 = (bf16[64,2,24,1]{0,2,3,1:T(8,128)(2,1)S(1)}, bf16[64,2,24,1]{0,2,3,1:T(8,128)(2,1)S(1)}, u32[]{:S(2)}, u32[]{:S(2)}) collective-permute-start(bf16[64,2,24,1]{0,2,3,1:T(8,128)(2,1)S(1)} %copy.31), channel_id=1, source_target_pairs={{0,1},{1,2},{2,3},{3,4},{4,5},{5,6},{6,7},{7,8},{8,9},{9,10},{10,1... | collective-permute-start | bytes 18440 | tf_op jit(solution)/shard_map/ppermute | solution.py:15
  13.4 3.2 %collective-permute-start.2 = (bf16[64,2,24,1]{0,2,3,1:T(8,128)(2,1)S(1)}, bf16[64,2,24,1]{0,2,3,1:T(8,128)(2,1)S(1)}, u32[]{:S(2)}, u32[]{:S(2)}) collective-permute-start(bf16[64,2,24,1]{0,2,3,1:T(8,128)(2,1)S(1)} %copy.32), channel_id=1, source_target_pairs={{1,0},{2,1},{3,2},{4,3},{5,4},{6,5},{7,6},{8,7},{9,8},{10,9},{11,1... | collective-permute-start | bytes 18440 | tf_op jit(solution)/shard_map/ppermute | solution.py:17
  13.7 19.1 %collective-permute-start = (bf16[64,2,24,128]{3,2,1,0:T(8,128)(2,1)S(1)}, bf16[64,2,24,128]{3,2,1,0:T(8,128)(2,1)}, u32[]{:S(2)}, u32[]{:S(2)}) collective-permute-start(bf16[64,2,24,128]{3,2,1,0:T(8,128)(2,1)S(1)} %copy-done.5), channel_id=1, source_target_pairs={{32,0},{64,32},{96,64},{128,96},{160,128},{192,160},{224,192},{33,... | collective-permute-start | bytes 2359304 | tf_op jit(solution)/shard_map/ppermute | solution.py:27
  20.0 1.8 copy-start.9
  26.7 31.5 %collective-permute-start.5 = (bf16[64,2,24,128]{3,0,2,1:T(8,128)(2,1)}, bf16[64,2,24,128]{3,0,2,1:T(8,128)(2,1)}, u32[]{:S(2)}, u32[]{:S(2)}) collective-permute-start(bf16[64,2,24,128]{3,0,2,1:T(8,128)(2,1)} %copy.24), channel_id=1, source_target_pairs={{0,32},{32,64},{64,96},{96,128},{128,160},{160,192},{192,224},{1,3... | collective-permute-start | bytes 2359304 | tf_op jit(solution)/shard_map/ppermute | solution.py:27
  32.7 1.1 copy-start.11
  36.6 3.0 copy-start.3
  40.0 0.7 copy-start.10
  41.4 8.7 %collective-permute-start.3 = (bf16[64,2,24,1]{0,2,3,1:T(8,128)(2,1)S(1)}, bf16[64,2,24,1]{0,2,3,1:T(8,128)(2,1)S(1)}, u32[]{:S(2)}, u32[]{:S(2)}) collective-permute-start(bf16[64,2,24,1]{0,2,3,1:T(8,128)(2,1)S(1)} %copy.33), channel_id=1, source_target_pairs={{0,1},{1,2},{2,3},{3,4},{4,5},{5,6},{6,7},{7,8},{8,9},{9,10},{10,1... | collective-permute-start | bytes 18440 | tf_op jit(solution)/shard_map/ppermute | solution.py:15
  47.9 3.5 %collective-permute-start.4 = (bf16[64,2,24,1]{0,2,3,1:T(8,128)(2,1)S(1)}, bf16[64,2,24,1]{0,2,3,1:T(8,128)(2,1)S(1)}, u32[]{:S(2)}, u32[]{:S(2)}) collective-permute-start(bf16[64,2,24,1]{0,2,3,1:T(8,128)(2,1)S(1)} %copy.34), channel_id=1, source_target_pairs={{1,0},{2,1},{3,2},{4,3},{5,4},{6,5},{7,6},{8,7},{9,8},{10,9},{11,1... | collective-permute-start | bytes 18440 | tf_op jit(solution)/shard_map/ppermute | solution.py:17
  50.8 1.3 copy-start.1
  52.0 0.9 copy-start.2
  54.9 3.3 %copy-start.6 = (bf16[64,2,24,128]{3,2,1,0:T(8,128)(2,1)S(1)}, bf16[64,2,24,128]{3,2,1,0:T(8,128)(2,1)}, u32[]{:S(2)}) copy-start(bf16[64,2,24,128]{3,2,1,0:T(8,128)(2,1)} %param.5) | copy-start | bytes 2359300
  146.7 1.1 copy-start.8
  147.8 1.1 copy-start.4
  148.9 1.1 copy-start.7
Sparse Core Ops, SparseCore 0:
  50.2 250.8 all-reduce.3
where the time goes:
time: 310 us
  waiting for transfers between devices  149 us (48%)
  blocking collectives  82.8 us (27%)
  matrix products  18.4 us (6%)
  local copies, waits for them, and re-layouts  17.8 us (6%)
  starting transfers between devices  16.4 us (5%)
  between operations  14.5 us (5%)
  other arithmetic  10.8 us (3%)
    psum x1, waiting for transfers between devices, body(): grad_sp, grad_tm = lax.psum((grad_sp, grad_tm), ('tm', 'lon'))  148 us
    psum x1, blocking collectives, body(): grad_sp, grad_tm = lax.psum((grad_sp, grad_tm), ('tm', 'lon'))  82.8 us
    ppermute x2, starting transfers between devices, padded_2(): lax.ppermute(tail, axis, [(i, (i + 1) % count) for i in range(count)])  8.86 us
    unnamed x32, local copies, waits for them, and re-layouts  8.46 us
    concatenate x4, other arithmetic, padded_2(): jnp.concatenate([lax.ppermute(tail, axis, [(i, (i + 1) % count) for i in...  8.03 us
    ppermute x2, starting transfers between devices, from_behind(): lax.ppermute(value, axis, [(source, source + steps) for source in range(f...  7.12 us
  transfers between devices with their start and end apart: 7, of which 3 were waited for; matrix products, arithmetic and copies ran while one was open for 13% of the time, Pallas kernels for 0%

commit v1 on v0

--- a/solution.py
+++ b/solution.py
@@ -90,7 +90,7 @@
             )
             back = term if back is None else back + term
     grad_frames = back.astype(jnp.bfloat16).reshape(channels, frame_count, lat_rows, lon_cols)
-    grad_sp, grad_tm = lax.psum((grad_sp, grad_tm), ("tm", "lon"))
+    grad_sp, grad_tm = lax.psum(lax.psum((grad_sp, grad_tm), "lon"), "tm")
     total_cells = frame_count * lax.axis_size("tm") * lat_rows * lon_cols * lax.axis_size("lon")
     scale = 1.0 / math.sqrt(total_cells)
     return (grad_frames, grad_sp * scale, grad_tm * scale)

time: 310 us -> 358 us (1.15); the launches traced: 310 us -> 353 us
  blocking collectives: 82.8 us -> 143 us
  waiting for transfers between devices: 149 us -> 132 us
    psum x1 -> x2, blocking collectives: 82.8 us -> 143 us  [body(): grad_sp, grad_tm = lax.psum(lax.psum((grad_sp, grad_tm), 'lon'), 'tm')]
    psum x1 -> x2, waiting for transfers between devices: 148 us -> 131 us  [body(): grad_sp, grad_tm = lax.psum(lax.psum((grad_sp, grad_tm), 'lon'), 'tm')]
    unnamed x32 -> x34, local copies, waits for them, and re-layouts: 8.46 us -> 8.47 us
  transfers between devices with their start and end apart: 7 -> 8, of which waited for: 3 -> 4; matrix products, arithmetic and copies ran while one was open for 13% -> 11% of each run, Pallas kernels for 0% -> 0%
where the time goes in v1:
time: 358 us; the launch traced here: 353 us
  blocking collectives  143 us (40%)
  waiting for transfers between devices  132 us (37%)
  local copies, waits for them, and re-layouts  18.6 us (5%)
  matrix products  18.5 us (5%)
  starting transfers between devices  16.4 us (5%)
  between operations  14.6 us (4%)
  other arithmetic  10.8 us (3%)
    psum x2, blocking collectives, body(): grad_sp, grad_tm = lax.psum(lax.psum((grad_sp, grad_tm), 'lon'), 'tm')  143 us
    psum x2, waiting for transfers between devices, body(): grad_sp, grad_tm = lax.psum(lax.psum((grad_sp, grad_tm), 'lon'), 'tm')  131 us
    ppermute x2, starting transfers between devices, padded_2(): lax.ppermute(tail, axis, [(i, (i + 1) % count) for i in range(count)])  8.87 us
    unnamed x34, local copies, waits for them, and re-layouts  8.47 us
    concatenate x4, other arithmetic, padded_2(): jnp.concatenate([lax.ppermute(tail, axis, [(i, (i + 1) % count) for i in...  8.02 us
  transfers between devices with their start and end apart: 8, of which 4 were waited for; matrix products, arithmetic and copies ran while one was open for 11% of the time, Pallas kernels for 0%

profile of v1, /device:TPU:1, one launch (start us, length us, event | category | flops | bytes accessed | tf_op | source)
XLA Modules:
  0.0 353.3 jit_solution(12531043543133433257)
XLA Ops:
  7.2 1.7 fusion.141
  9.0 0.7 copy.31
  9.7 3.1 collective-permute-start.1
  12.7 0.7 copy.32
  13.7 1.5 collective-permute-start
  15.2 0.7 copy.14
  15.9 0.7 collective-permute-done.2
  16.6 0.7 copy.15
  17.3 1.9 fusion.13
  19.1 0.9 pad_maximum_fusion.3
  20.0 1.8 fusion.139
  24.7 0.8 multiply_convert_fusion
  25.6 1.1 copy.24
  26.7 5.6 %collective-permute-start.5 = (bf16[64,2,24,128]{3,0,2,1:T(8,128)(2,1)}, bf16[64,2,24,128]{3,0,2,1:T(8,128)(2,1)}, u32[]{:S(2)}, u32[]{:S(2)}) collective-permute-start(bf16[64,2,24,128]{3,0,2,1:T(8,128)(2,1)} %copy.24), channel_id=1, source_target_pairs={{0,32},{32,64},{64,96},{96,128},{128,160},{160,192},{192,224},{1,3... | collective-permute-start | bytes 2359304 | tf_op jit(solution)/shard_map/ppermute | solution.py:27
  32.8 1.1 pad_maximum_fusion.4
  33.8 0.4 convolution_bitcast_fusion.4
  34.7 1.9 fusion.7
  40.0 0.7 copy-done.11
  40.7 0.7 copy.33
  41.4 5.8 %collective-permute-start.3 = (bf16[64,2,24,1]{0,2,3,1:T(8,128)(2,1)S(1)}, bf16[64,2,24,1]{0,2,3,1:T(8,128)(2,1)S(1)}, u32[]{:S(2)}, u32[]{:S(2)}) collective-permute-start(bf16[64,2,24,1]{0,2,3,1:T(8,128)(2,1)S(1)} %copy.33), channel_id=1, source_target_pairs={{0,1},{1,2},{2,3},{3,4},{4,5},{5,6},{6,7},{7,8},{8,9},{9,10},{10,1... | collective-permute-start | bytes 18440 | tf_op jit(solution)/shard_map/ppermute | solution.py:15
  47.2 0.7 copy.34
  48.0 2.1 fusion.19
  50.2 0.7 copy.20
  50.8 0.5 collective-permute-done.4
  51.3 0.7 copy.21
  52.0 0.9 copy-done.2
  52.9 2.0 pad_maximum_fusion
  54.9 3.3 select_maximum_fusion
  58.2 1.5 fusion.28
  59.7 1.5 convolution_bitcast_fusion.5
  61.3 105.4 %psum.30 = f32[3,64,64]{1,2,0:T(8,128)S(1)} all-reduce(f32[3,64,64]{1,2,0:T(8,128)S(1)} %pad_maximum_fusion.5), channel_id=1, replica_groups=mesh['tm'=8,'lon'=32] {'lon'}, use_global_device_ids=true, to_apply=%region_2.3 | all-reduce | flops 12288 | bytes 98304 | tf_op jit(solution)/shard_map/psum | solution.py:93
  166.7 37.3 %psum.31 = f32[3,64,64]{1,2,0:T(8,128)S(1)} all-reduce(f32[3,64,64]{1,2,0:T(8,128)S(1)} %psum.30), channel_id=1, replica_groups=mesh['tm'=8,'lon'=32] {'tm'}, use_global_device_ids=true, to_apply=%region_3.4 | all-reduce | flops 12288 | bytes 98304 | tf_op jit(solution)/shard_map/psum | solution.py:93
  203.9 2.6 fusion.138
  206.9 0.4 convolution_add_fusion.10
  207.4 0.4 convolution_add_fusion.9
  207.8 0.7 copy-done.9
  208.5 0.4 convolution_add_fusion.8
  208.9 0.7 copy-done.5
  210.0 0.7 copy-done.8
  210.7 0.4 convolution_add_fusion.6
  211.2 0.4 convolution_add_fusion.5
  211.6 0.4 convolution_add_fusion.4
  212.0 0.7 copy.28
  212.8 47.1 %all-reduce.5.cloned.1.call-done = f32[3,3,64,64]{3,2,1,0:T(8,128)} async-done(((f32[3,3,64,64]{3,2,1,0:T(8,128)}), f32[3,3,64,64]{3,2,1,0:T(8,128)}) %all-reduce.5.cloned.1.call-update) | async-done | bytes 147472 | tf_op jit(solution)/shard_map/psum | solution.py:93
  259.9 0.4 fusion.18
  260.4 1.0 copy.56
  261.4 83.4 %all-reduce.7.cloned.1.call-done = f32[3,3,64,64]{3,2,1,0:T(8,128)} async-done(((f32[3,3,64,64]{3,2,1,0:T(8,128)}), f32[3,3,64,64]{3,2,1,0:T(8,128)}) %all-reduce.7.cloned.1.call-update) | async-done | bytes 147472 | tf_op jit(solution)/shard_map/psum | solution.py:93
  344.8 1.7 broadcast_multiply_fusion
  (56 shorter events, 8.4 us)
Async XLA Ops:
  7.2 252.8 %all-reduce.5.cloned.1.call-start = ((), (), s32[]{:S(2)}) async-start(), calls=%async_computation | async-start | bytes 589824 | tf_op jit(solution)/shard_map/psum | solution.py:93
  8.9 4.8 %copy-start.6 = (bf16[64,2,24,128]{3,2,1,0:T(8,128)(2,1)S(1)}, bf16[64,2,24,128]{3,2,1,0:T(8,128)(2,1)}, u32[]{:S(2)}) copy-start(bf16[64,2,24,128]{3,2,1,0:T(8,128)(2,1)} %param.5) | copy-start | bytes 2359300
  9.0 8.3 %copy-start = (bf16[64,2,24,128]{3,2,1,0:T(8,128)(2,1)S(1)}, bf16[64,2,24,128]{3,2,1,0:T(8,128)(2,1)}, u32[]{:S(2)}) copy-start(bf16[64,2,24,128]{3,2,1,0:T(8,128)(2,1)} %param.4) | copy-start | bytes 2359300
  9.7 5.5 %collective-permute-start.1 = (bf16[64,2,24,1]{0,2,3,1:T(8,128)(2,1)S(1)}, bf16[64,2,24,1]{0,2,3,1:T(8,128)(2,1)S(1)}, u32[]{:S(2)}, u32[]{:S(2)}) collective-permute-start(bf16[64,2,24,1]{0,2,3,1:T(8,128)(2,1)S(1)} %copy.31), channel_id=1, source_target_pairs={{0,1},{1,2},{2,3},{3,4},{4,5},{5,6},{6,7},{7,8},{8,9},{9,10},{10,1... | collective-permute-start | bytes 18440 | tf_op jit(solution)/shard_map/ppermute | solution.py:15
  13.4 3.2 collective-permute-start.2
  13.7 19.0 %collective-permute-start = (bf16[64,2,24,128]{3,2,1,0:T(8,128)(2,1)S(1)}, bf16[64,2,24,128]{3,2,1,0:T(8,128)(2,1)}, u32[]{:S(2)}, u32[]{:S(2)}) collective-permute-start(bf16[64,2,24,128]{3,2,1,0:T(8,128)(2,1)S(1)} %copy-done.6), channel_id=1, source_target_pairs={{32,0},{64,32},{96,64},{128,96},{160,128},{192,160},{224,192},{33,... | collective-permute-start | bytes 2359304 | tf_op jit(solution)/shard_map/ppermute | solution.py:27
  20.0 1.8 copy-start.10
  26.7 31.5 %collective-permute-start.5 = (bf16[64,2,24,128]{3,0,2,1:T(8,128)(2,1)}, bf16[64,2,24,128]{3,0,2,1:T(8,128)(2,1)}, u32[]{:S(2)}, u32[]{:S(2)}) collective-permute-start(bf16[64,2,24,128]{3,0,2,1:T(8,128)(2,1)} %copy.24), channel_id=1, source_target_pairs={{0,32},{32,64},{64,96},{96,128},{128,160},{160,192},{192,224},{1,3... | collective-permute-start | bytes 2359304 | tf_op jit(solution)/shard_map/ppermute | solution.py:27
  32.7 1.1 copy-start.12
  36.6 3.0 copy-start.4
  40.0 0.7 copy-start.11
  41.4 8.7 %collective-permute-start.3 = (bf16[64,2,24,1]{0,2,3,1:T(8,128)(2,1)S(1)}, bf16[64,2,24,1]{0,2,3,1:T(8,128)(2,1)S(1)}, u32[]{:S(2)}, u32[]{:S(2)}) collective-permute-start(bf16[64,2,24,1]{0,2,3,1:T(8,128)(2,1)S(1)} %copy.33), channel_id=1, source_target_pairs={{0,1},{1,2},{2,3},{3,4},{4,5},{5,6},{6,7},{7,8},{8,9},{9,10},{10,1... | collective-permute-start | bytes 18440 | tf_op jit(solution)/shard_map/ppermute | solution.py:15
  47.9 3.5 collective-permute-start.4
  50.1 294.7 %all-reduce.7.cloned.1.call-start = ((), (), s32[]{:S(2)}) async-start(), calls=%async_computation.1 | async-start | bytes 589824 | tf_op jit(solution)/shard_map/psum | solution.py:93
  50.8 1.2 copy-start.1
  52.0 0.9 copy-start.2
  54.9 3.3 copy-start.7
  207.3 1.1 copy-start.9
  208.5 1.1 copy-start.5
  209.6 1.1 copy-start.8
  211.6 48.4 %copy-start.3 = (bf16[64,2,24,128]{3,2,1,0:T(8,128)(2,1)S(1)}, bf16[64,2,24,128]{3,2,1,0:T(8,128)(2,1)}, u32[]{:S(2)}) copy-start(bf16[64,2,24,128]{3,2,1,0:T(8,128)(2,1)} %get-tuple-element.9) | copy-start | bytes 2359300
Sparse Core Ops, SparseCore 0:
  50.2 209.6 all-reduce.4
  262.7 81.9 all-reduce.6
